TPU v7x, 256 devices: a whole 4x4x8 slice. The times are simulated.
256 devices in a mesh: dist: 16 (over z_lo, y), rows: 16 (over z_hi, x, core).
Axes of the slice: x: 4, y: 4, z: 8 (z_hi: 2, z_lo: 4; z = z_hi * 4 + z_lo), core: 2. Of those that a mesh axis runs over, the one named last changes fastest.
Arguments:
- wave: float32 [16, 2, 2048, 2048], P('dist', None, 'rows'), may hold values from -6 to 6
- object_slice: float32 [2, 2048, 2048], P(None, 'rows', 'dist'), may hold values from 0 to 1.5
- fresnel: float32 [16], P('dist'), may hold values from 256 to 1024
Outputs:
- detected: float32 [16, 2, 2048, 2048], P('dist', None, 'rows')
All inputs are finite; a program needn't handle non-finite values.
Results may differ from a plain program's by a relative error of at most 0.00035.
Values sent between devices are 32-bit elements; how exact they have to be, the bound alone decides.
A program may use at most 64 MiB of HBM per device.

v0:
```python
import math
import jax
import jax.numpy as jnp
from jax import lax
from jax.sharding import PartitionSpec as P

highest = lax.Precision.HIGHEST


def swapped(shard, axis, apart):
    return lax.ppermute(shard, axis, [(i, i ^ 1 << apart) for i in range(lax.axis_size(axis))])


def angle_table(period, direction, row_count, col_count):
    row_grid = lax.broadcasted_iota(jnp.int32, (row_count, col_count), 0)
    col_grid = lax.broadcasted_iota(jnp.int32, (row_count, col_count), 1)
    phase_angle = (
        direction * 2.0 * math.pi / period * (row_grid * col_grid % period).astype(jnp.float32)
    )
    return (jnp.cos(phase_angle), jnp.sin(phase_angle))


def complex_mix(form, real_part, imag_part, table_re, table_im):
    out_re = jnp.einsum(form, real_part, table_re, precision=highest) - jnp.einsum(
        form, imag_part, table_im, precision=highest
    )
    out_im = jnp.einsum(form, real_part, table_im, precision=highest) + jnp.einsum(
        form, imag_part, table_re, precision=highest
    )
    return (out_re, out_im)


def split_length(length):
    levels = length.bit_length() - 1
    outer_len = 1 << (levels + 1) // 2
    return (outer_len, length // outer_len)


def transform_last(real_part, imag_part, direction):
    length = real_part.shape[-1]
    outer_len, inner_len = split_length(length)
    leading = real_part.shape[:-1]
    real_part = real_part.reshape(leading + (outer_len, inner_len))
    imag_part = imag_part.reshape(leading + (outer_len, inner_len))
    first_re, first_im = angle_table(outer_len, direction, outer_len, outer_len)
    real_part, imag_part = complex_mix("...ab,ae->...eb", real_part, imag_part, first_re, first_im)
    twiddle_re, twiddle_im = angle_table(length, direction, outer_len, inner_len)
    real_part, imag_part = (
        real_part * twiddle_re - imag_part * twiddle_im,
        real_part * twiddle_im + imag_part * twiddle_re,
    )
    last_re, last_im = angle_table(inner_len, direction, inner_len, inner_len)
    real_part, imag_part = complex_mix("...eb,bd->...de", real_part, imag_part, last_re, last_im)
    return (real_part.reshape(leading + (length,)), imag_part.reshape(leading + (length,)))


def signed_frequency(index_line, length):
    return (
        jnp.where(index_line < length // 2, index_line, index_line - length).astype(jnp.float32)
        / length
    )


def apply_kernel(real_part, imag_part, fresnel, row_index, col_index, length):
    row_freq = signed_frequency(row_index, length)
    col_freq = signed_frequency(col_index, length)
    freq_sum = row_freq[:, None] ** 2 + col_freq[None, :] ** 2
    phase_angle = (-math.pi * fresnel)[:, None, None] * freq_sum[None]
    kernel_re = jnp.cos(phase_angle)
    kernel_im = jnp.sin(phase_angle)
    return (
        real_part * kernel_re - imag_part * kernel_im,
        real_part * kernel_im + imag_part * kernel_re,
    )


def body(wave, object_slice, fresnel):
    row_count = wave.shape[2]
    length = wave.shape[3]
    group_size = lax.axis_size("rows")
    position = lax.axis_index("rows")
    slice_piece = lax.all_gather(object_slice, "dist", axis=2, tiled=True)
    amplitude = jnp.exp(-slice_piece[1])
    trans_re = amplitude * jnp.cos(slice_piece[0])
    trans_im = amplitude * jnp.sin(slice_piece[0])
    wave_re = wave[:, 0]
    wave_im = wave[:, 1]
    exited = jnp.stack(
        (wave_re * trans_re - wave_im * trans_im, wave_re * trans_im + wave_im * trans_re), axis=1
    )
    real_part, imag_part = transform_last(exited[:, 0], exited[:, 1], -1.0)
    rounds = group_size.bit_length() - 1
    for level in reversed(range(rounds)):
        stride = 1 << level
        partner = swapped(jnp.stack((real_part, imag_part), axis=1), "rows", level)
        upper_flag = (position // stride % 2).astype(jnp.float32)
        within = (position % stride).astype(jnp.float32)
        phase_angle = -2.0 * math.pi / (2 * stride) * within
        factor_re = 1.0 - upper_flag + upper_flag * jnp.cos(phase_angle)
        factor_im = upper_flag * jnp.sin(phase_angle)
        own_sign = 1.0 - 2.0 * upper_flag
        summed_re = partner[:, 0] + own_sign * real_part
        summed_im = partner[:, 1] + own_sign * imag_part
        real_part = summed_re * factor_re - summed_im * factor_im
        imag_part = summed_re * factor_im + summed_im * factor_re
    bit_reverse = jnp.zeros((), jnp.int32)
    for level in range(rounds):
        bit_reverse = bit_reverse + position // (1 << level) % 2 * (1 << rounds - 1 - level)
    local_rows = lax.iota(jnp.int32, row_count)
    shift_angle = -2.0 * math.pi / length * (local_rows * bit_reverse % length).astype(jnp.float32)
    shift_re = jnp.cos(shift_angle)[:, None]
    shift_im = jnp.sin(shift_angle)[:, None]
    real_part, imag_part = (
        real_part * shift_re - imag_part * shift_im,
        real_part * shift_im + imag_part * shift_re,
    )
    local_re, local_im = angle_table(row_count, -1.0, row_count, row_count)
    real_part, imag_part = complex_mix("...lc,lm->...mc", real_part, imag_part, local_re, local_im)
    row_index = bit_reverse + group_size * local_rows
    col_index = lax.iota(jnp.int32, length)
    real_part, imag_part = apply_kernel(real_part, imag_part, fresnel, row_index, col_index, length)
    back_re, back_im = angle_table(row_count, 1.0, row_count, row_count)
    real_part, imag_part = complex_mix("...lc,lm->...mc", real_part, imag_part, back_re, back_im)
    real_part = real_part / row_count
    imag_part = imag_part / row_count
    real_part, imag_part = (
        real_part * shift_re + imag_part * shift_im,
        imag_part * shift_re - real_part * shift_im,
    )
    for level in range(rounds):
        stride = 1 << level
        partner = swapped(jnp.stack((real_part, imag_part), axis=1), "rows", level)
        upper_flag = (position // stride % 2).astype(jnp.float32)
        within = (position % stride).astype(jnp.float32)
        phase_angle = 2.0 * math.pi / (2 * stride) * within
        turn_re = jnp.cos(phase_angle)
        turn_im = jnp.sin(phase_angle)
        lower_flag = 1.0 - upper_flag
        second_re = upper_flag * real_part + lower_flag * partner[:, 0]
        second_im = upper_flag * imag_part + lower_flag * partner[:, 1]
        first_re = upper_flag * partner[:, 0] + lower_flag * real_part
        first_im = upper_flag * partner[:, 1] + lower_flag * imag_part
        turned_re = second_re * turn_re - second_im * turn_im
        turned_im = second_re * turn_im + second_im * turn_re
        own_sign = 1.0 - 2.0 * upper_flag
        real_part = 0.5 * (first_re + own_sign * turned_re)
        imag_part = 0.5 * (first_im + own_sign * turned_im)
    real_part, imag_part = transform_last(real_part, imag_part, 1.0)
    real_part = real_part / length
    imag_part = imag_part / length
    return jnp.stack((real_part, imag_part), axis=1)


def solution(mesh):
    return jax.shard_map(
        body,
        mesh=mesh,
        in_specs=(P("dist", None, "rows", None), P(None, "rows", "dist"), P("dist")),
        out_specs=P("dist", None, "rows", None),
        check_vma=False,
    )
```

profile of v0, /device:TPU:97, one launch (start us, length us, event | category | flops | bytes accessed | tf_op | source)
XLA Modules:
  0.0 554.5 jit_solution(11762353641238578681)
XLA Ops:
  6.5 1.7 copy.21
  8.3 1.7 fusion.252
  10.7 67.3 %all-gather.2.cloned.1.call-done = f32[2,128,2048]{1,2,0:T(8,128)} async-done(((f32[2,128,128]{1,2,0:T(8,128)}), f32[2,128,2048]{1,2,0:T(8,128)}) %all-gather.2.cloned.1.call-update) | async-done | bytes 2097168 | tf_op jit(solution)/shard_map/all_gather | solution.py:82
  78.0 5.1 fusion.24
  83.1 1.7 fusion.47
  84.7 1.6 fusion.49
  86.4 1.7 fusion.8
  88.0 2.2 add_bitcast_fusion.1
  90.2 1.6 fusion.41
  91.8 1.6 fusion.43
  93.4 2.6 broadcast_multiply_fusion
  96.0 1.7 copy.32
  97.8 1.6 copy.34
  99.4 2.7 broadcast_multiply_fusion.1
  104.4 4.2 collective-permute-start
  108.7 88.3 %collective-permute-done = f32[1,2,128,2048]{3,2,1,0:T(8,128)} collective-permute-done((f32[1,2,128,2048]{3,2,1,0:T(8,128)}, f32[1,2,128,2048]{3,2,1,0:T(8,128)}, u32[]{:S(2)}, u32[]{:S(2)}) %collective-permute-start) | collective-permute-done | bytes 2097184 | tf_op jit(solution)/shard_map/ppermute | solution.py:11
  197.0 1.9 multiply_add_fusion.10
  199.9 2.6 collective-permute-start.1
  202.7 40.7 %collective-permute-done.1 = f32[1,2,128,2048]{3,2,1,0:T(8,128)} collective-permute-done((f32[1,2,128,2048]{3,2,1,0:T(8,128)S(1)}, f32[1,2,128,2048]{3,2,1,0:T(8,128)}, u32[]{:S(2)}, u32[]{:S(2)}) %collective-permute-start.1) | collective-permute-done | bytes 2097184 | tf_op jit(solution)/shard_map/ppermute | solution.py:11
  243.5 2.3 multiply_add_fusion.7
  248.6 39.9 %collective-permute-done.2 = f32[1,2,128,2048]{3,2,1,0:T(8,128)} collective-permute-done((f32[1,2,128,2048]{3,2,1,0:T(8,128)}, f32[1,2,128,2048]{3,2,1,0:T(8,128)}, u32[]{:S(2)}, u32[]{:S(2)}) %collective-permute-start.2) | collective-permute-done | bytes 2097184 | tf_op jit(solution)/shard_map/ppermute | solution.py:11
  288.5 1.9 multiply_subtract_fusion.4
  292.0 7.2 %collective-permute-start.3 = (f32[1,2,128,2048]{3,2,1,0:T(8,128)}, f32[1,2,128,2048]{3,2,1,0:T(8,128)}, u32[]{:S(2)}, u32[]{:S(2)}) collective-permute-start(f32[1,2,128,2048]{3,2,1,0:T(8,128)} %pad_maximum_fusion.3), channel_id=1, source_target_pairs={{0,1},{1,0},{2,3},{3,2},{4,5},{5,4},{6,7},{7,6},{8,9},{9,8},{10,11... | collective-permute-start | bytes 6291464 | tf_op jit(solution)/shard_map/ppermute | solution.py:11
  302.2 2.8 bitcast_add_fusion.20
  305.0 2.4 fusion.11
  315.1 5.5 fusion.57
  320.6 5.0 fusion.56
  325.6 5.2 convolution_subtract_fusion
  330.8 5.3 multiply_add_fusion
  336.4 4.1 collective-permute-done.4
  344.3 46.0 %collective-permute-done.5 = f32[1,2,128,2048]{3,2,1,0:T(8,128)} collective-permute-done((f32[1,2,128,2048]{3,2,1,0:T(8,128)}, f32[1,2,128,2048]{3,2,1,0:T(8,128)}, u32[]{:S(2)}, u32[]{:S(2)}) %collective-permute-start.5) | collective-permute-done | bytes 2097184 | tf_op jit(solution)/shard_map/ppermute | solution.py:11
  390.3 3.4 multiply_bitcast_fusion.3
  395.2 2.7 collective-permute-start.6
  398.0 45.1 %collective-permute-done.6 = f32[1,2,128,2048]{3,2,1,0:T(8,128)S(1)} collective-permute-done((f32[1,2,128,2048]{3,2,1,0:T(8,128)}, f32[1,2,128,2048]{3,2,1,0:T(8,128)S(1)}, u32[]{:S(2)}, u32[]{:S(2)}) %collective-permute-start.6) | collective-permute-done | bytes 2097184 | tf_op jit(solution)/shard_map/ppermute | solution.py:11
  444.4 2.7 multiply_bitcast_fusion.1
  448.5 3.6 collective-permute-start.7
  452.4 70.4 %collective-permute-done.7 = f32[1,2,128,2048]{3,2,1,0:T(8,128)} collective-permute-done((f32[1,2,128,2048]{3,2,1,0:T(8,128)}, f32[1,2,128,2048]{3,2,1,0:T(8,128)}, u32[]{:S(2)}, u32[]{:S(2)}) %collective-permute-start.7) | collective-permute-done | bytes 2097184 | tf_op jit(solution)/shard_map/ppermute | solution.py:11
  522.8 3.3 fusion.14
  526.1 1.5 copy.41
  527.7 2.6 fusion.37
  530.3 1.7 fusion.35
  532.3 2.9 fusion.5
  535.2 2.1 add_bitcast_fusion
  537.3 1.6 fusion.31
  539.0 1.6 fusion.29
  540.6 1.8 fusion.3
  543.0 1.6 fusion.1
  545.4 1.8 copy.53
  (46 shorter events, 28.2 us)
Async XLA Ops:
  6.5 71.5 %all-gather.2.cloned.1.call-start = ((), (), s32[]{:S(2)}) async-start(), calls=%async_computation | async-start | bytes 2228224 | tf_op jit(solution)/shard_map/all_gather | solution.py:82
  104.4 92.6 %collective-permute-start = (f32[1,2,128,2048]{3,2,1,0:T(8,128)}, f32[1,2,128,2048]{3,2,1,0:T(8,128)}, u32[]{:S(2)}, u32[]{:S(2)}) collective-permute-start(f32[1,2,128,2048]{3,2,1,0:T(8,128)} %pad_maximum_fusion), channel_id=1, source_target_pairs={{0,8},{1,9},{2,10},{3,11},{4,12},{5,13},{6,14},{7,15},{8,0},{9,1},... | collective-permute-start | bytes 6291464 | tf_op jit(solution)/shard_map/ppermute | solution.py:11
  198.9 1.0 copy-start
  199.9 43.5 %collective-permute-start.1 = (f32[1,2,128,2048]{3,2,1,0:T(8,128)S(1)}, f32[1,2,128,2048]{3,2,1,0:T(8,128)}, u32[]{:S(2)}, u32[]{:S(2)}) collective-permute-start(f32[1,2,128,2048]{3,2,1,0:T(8,128)S(1)} %pad_maximum_fusion.1), channel_id=1, source_target_pairs={{0,4},{1,5},{2,6},{3,7},{4,0},{5,1},{6,2},{7,3},{8,12},{9,13},{10,... | collective-permute-start | bytes 6291464 | tf_op jit(solution)/shard_map/ppermute | solution.py:11
  247.2 41.3 %collective-permute-start.2 = (f32[1,2,128,2048]{3,2,1,0:T(8,128)}, f32[1,2,128,2048]{3,2,1,0:T(8,128)}, u32[]{:S(2)}, u32[]{:S(2)}) collective-permute-start(f32[1,2,128,2048]{3,2,1,0:T(8,128)} %pad_maximum_fusion.2), channel_id=1, source_target_pairs={{0,2},{1,3},{2,0},{3,1},{4,6},{5,7},{6,4},{7,5},{8,10},{9,11},{10,... | collective-permute-start | bytes 6291464 | tf_op jit(solution)/shard_map/ppermute | solution.py:11
  290.5 9.5 %copy-start.1 = (f32[1,128,32,64]{1,2,3,0:T(8,128)S(1)}, f32[1,128,32,64]{1,2,3,0:T(8,128)}, u32[]{:S(2)}) copy-start(f32[1,128,32,64]{1,2,3,0:T(8,128)} %get-tuple-element.48) | copy-start | bytes 3145732
  292.0 13.1 %collective-permute-start.3 = (f32[1,2,128,2048]{3,2,1,0:T(8,128)}, f32[1,2,128,2048]{3,2,1,0:T(8,128)}, u32[]{:S(2)}, u32[]{:S(2)}) collective-permute-start(f32[1,2,128,2048]{3,2,1,0:T(8,128)} %pad_maximum_fusion.3), channel_id=1, source_target_pairs={{0,1},{1,0},{2,3},{3,2},{4,5},{5,4},{6,7},{7,6},{8,9},{9,8},{10,11... | collective-permute-start | bytes 6291464 | tf_op jit(solution)/shard_map/ppermute | solution.py:11
  300.0 1.2 copy-start.2
  336.3 4.2 collective-permute-start.4
  342.9 47.4 %collective-permute-start.5 = (f32[1,2,128,2048]{3,2,1,0:T(8,128)}, f32[1,2,128,2048]{3,2,1,0:T(8,128)}, u32[]{:S(2)}, u32[]{:S(2)}) collective-permute-start(f32[1,2,128,2048]{3,2,1,0:T(8,128)} %pad_maximum_fusion.5), channel_id=1, source_target_pairs={{0,2},{1,3},{2,0},{3,1},{4,6},{5,7},{6,4},{7,5},{8,10},{9,11},{10,... | collective-permute-start | bytes 6291464 | tf_op jit(solution)/shard_map/ppermute | solution.py:11
  395.2 47.9 %collective-permute-start.6 = (f32[1,2,128,2048]{3,2,1,0:T(8,128)}, f32[1,2,128,2048]{3,2,1,0:T(8,128)S(1)}, u32[]{:S(2)}, u32[]{:S(2)}) collective-permute-start(f32[1,2,128,2048]{3,2,1,0:T(8,128)} %pad_maximum_fusion.6), channel_id=1, source_target_pairs={{0,4},{1,5},{2,6},{3,7},{4,0},{5,1},{6,2},{7,3},{8,12},{9,13},{10,... | collective-permute-start | bytes 6291464 | tf_op jit(solution)/shard_map/ppermute | solution.py:11
  443.1 1.3 copy-start.3
  448.5 74.2 %collective-permute-start.7 = (f32[1,2,128,2048]{3,2,1,0:T(8,128)}, f32[1,2,128,2048]{3,2,1,0:T(8,128)}, u32[]{:S(2)}, u32[]{:S(2)}) collective-permute-start(f32[1,2,128,2048]{3,2,1,0:T(8,128)} %pad_maximum_fusion.7), channel_id=1, source_target_pairs={{0,8},{1,9},{2,10},{3,11},{4,12},{5,13},{6,14},{7,15},{8,0},{9,1},... | collective-permute-start | bytes 6291464 | tf_op jit(solution)/shard_map/ppermute | solution.py:11
Sparse Core Ops, SparseCore 0:
  9.1 68.7 all-gather.1
where the time goes:
time: 565 us; the launch traced here: 555 us
  waiting for transfers between devices  402 us (71%)
  matrix products  58.6 us (10%)
  other arithmetic  37.9 us (7%)
  starting transfers between devices  22.9 us (4%)
  local copies, waits for them, and re-layouts  17.4 us (3%)
  between operations  15.9 us (3%)
    ppermute x8, waiting for transfers between devices, swapped(): lax.ppermute(shard, axis, [(i, i ^ 1 << apart) for i in range(lax.axis_si...  334 us
    all_gather x1, waiting for transfers between devices, body(): slice_piece = lax.all_gather(object_slice, 'dist', axis=2, tiled=True)  67.3 us
    ppermute x8, starting transfers between devices, swapped(): lax.ppermute(shard, axis, [(i, i ^ 1 << apart) for i in range(lax.axis_si...  22.9 us
    dot_general x6, matrix products, complex_mix(): jnp.einsum(form, imag_part, table_im, precision=highest)  16.3 us
    another operation x11, other arithmetic, body(): partner = swapped(jnp.stack((real_part, imag_part), axis=1), 'rows', level)  16.2 us
    dot_general x6, matrix products, complex_mix(): jnp.einsum(form, imag_part, table_re, precision=highest)  14.8 us
    dot_general x6, matrix products, complex_mix(): jnp.einsum(form, real_part, table_re, precision=highest)  14 us
    dot_general x6, matrix products, complex_mix(): jnp.einsum(form, real_part, table_im, precision=highest)  13.5 us
  transfers between devices with their start and end apart: 9, of which 8 were waited for; matrix products, arithmetic and copies ran while one was open for 1% of the time, Pallas kernels for 0%

commit v1 on v0

--- a/solution.py
+++ b/solution.py
@@ -79,7 +79,12 @@
     length = wave.shape[3]
     group_size = lax.axis_size("rows")
     position = lax.axis_index("rows")
-    slice_piece = lax.all_gather(object_slice, "dist", axis=2, tiled=True)
+    slice_piece = jnp.concatenate(
+        lax.all_to_all(
+            jnp.stack([object_slice for _ in range(lax.axis_size("dist"))], axis=0), "dist", 0, 0
+        ),
+        axis=2,
+    )
     amplitude = jnp.exp(-slice_piece[1])
     trans_re = amplitude * jnp.cos(slice_piece[0])
     trans_im = amplitude * jnp.sin(slice_piece[0])

time: 565 us -> 516 us (0.913)
  the two profiles are of different devices: /device:TPU:97 before, /device:TPU:52 now
where the time goes in v1:
time: 516 us; the launch traced here: 514 us
  waiting for transfers between devices  370 us (72%)
  matrix products  58.8 us (11%)
  other arithmetic  37.8 us (7%)
  local copies, waits for them, and re-layouts  23.2 us (4%)
  starting transfers between devices  21.7 us (4%)
    ppermute x8, waiting for transfers between devices, swapped(): lax.ppermute(shard, axis, [(i, i ^ 1 << apart) for i in range(lax.axis_si...  330 us
    all_to_all x1, waiting for transfers between devices, body(): lax.all_to_all(jnp.stack([object_slice for _ in range(lax.axis_size('dist...  40.3 us
    dot_general x6, matrix products, complex_mix(): jnp.einsum(form, imag_part, table_im, precision=highest)  16.3 us
    another operation x11, other arithmetic, body(): partner = swapped(jnp.stack((real_part, imag_part), axis=1), 'rows', level)  16.2 us
    dot_general x6, matrix products, complex_mix(): jnp.einsum(form, imag_part, table_re, precision=highest)  15 us
    dot_general x6, matrix products, complex_mix(): jnp.einsum(form, real_part, table_re, precision=highest)  14 us
    dot_general x6, matrix products, complex_mix(): jnp.einsum(form, real_part, table_im, precision=highest)  13.5 us
    ppermute x8, starting transfers between devices, swapped(): lax.ppermute(shard, axis, [(i, i ^ 1 << apart) for i in range(lax.axis_si...  13.3 us
  transfers between devices with their start and end apart: 9, of which 8 were waited for; matrix products, arithmetic and copies ran while one was open for 2% of the time, Pallas kernels for 0%

profile of v1, /device:TPU:52, one launch (start us, length us, event | category | flops | bytes accessed | tf_op | source)
XLA Modules:
  0.0 513.6 jit_solution(9474873127654218339)
XLA Ops:
  1.0 1.6 stack.36
  2.6 8.4 %all-to-all-start = ((f32[16,2,128,128]{2,3,1,0:T(8,128)}), f32[16,2,128,128]{2,3,1,0:T(8,128)S(1)}, u32[]{:S(2)}, u32[]{:S(2)}) async-start(f32[16,2,128,128]{2,3,1,0:T(8,128)} %stack.36), calls=%async_computation | async-start | bytes 4194304 | tf_op jit(solution)/shard_map/all_to_all | solution.py:83
  11.0 3.1 fusion.250
  14.1 1.5 copy.89
  15.6 2.5 copy.90
  18.3 40.3 %all-to-all-done = f32[16,2,128,128]{2,3,1,0:T(8,128)S(1)} async-done(((f32[16,2,128,128]{2,3,1,0:T(8,128)}), f32[16,2,128,128]{2,3,1,0:T(8,128)S(1)}, u32[]{:S(2)}, u32[]{:S(2)}) %all-to-all-start) | async-done | bytes 2097184 | tf_op jit(solution)/shard_map/all_to_all | solution.py:83
  58.7 4.4 cosine_multiply_fusion
  63.7 1.7 fusion.45
  65.4 1.6 fusion.47
  67.0 1.7 fusion.8
  68.7 2.2 add_bitcast_fusion.1
  70.8 1.6 fusion.39
  72.4 1.6 fusion.41
  74.0 2.8 broadcast_multiply_fusion
  76.9 1.6 copy.67
  78.4 1.6 copy.69
  80.0 2.7 broadcast_multiply_fusion.1
  85.1 4.4 collective-permute-start
  89.7 90.9 %collective-permute-done = f32[1,2,128,2048]{3,2,1,0:T(8,128)} collective-permute-done((f32[1,2,128,2048]{3,2,1,0:T(8,128)}, f32[1,2,128,2048]{3,2,1,0:T(8,128)}, u32[]{:S(2)}, u32[]{:S(2)}) %collective-permute-start) | collective-permute-done | bytes 2097184 | tf_op jit(solution)/shard_map/ppermute | solution.py:11
  180.6 1.9 multiply_add_fusion.10
  184.2 48.5 %collective-permute-done.1 = f32[1,2,128,2048]{3,2,1,0:T(8,128)} collective-permute-done((f32[1,2,128,2048]{3,2,1,0:T(8,128)S(1)}, f32[1,2,128,2048]{3,2,1,0:T(8,128)}, u32[]{:S(2)}, u32[]{:S(2)}) %collective-permute-start.1) | collective-permute-done | bytes 2097184 | tf_op jit(solution)/shard_map/ppermute | solution.py:11
  232.6 2.3 multiply_add_fusion.7
  237.7 45.7 %collective-permute-done.2 = f32[1,2,128,2048]{3,2,1,0:T(8,128)} collective-permute-done((f32[1,2,128,2048]{3,2,1,0:T(8,128)}, f32[1,2,128,2048]{3,2,1,0:T(8,128)}, u32[]{:S(2)}, u32[]{:S(2)}) %collective-permute-start.2) | collective-permute-done | bytes 2097184 | tf_op jit(solution)/shard_map/ppermute | solution.py:11
  283.4 1.9 multiply_subtract_fusion.4
  290.1 2.8 bitcast_add_fusion.20
  292.9 2.4 fusion.11
  303.0 5.5 %fusion.55 = f32[128,2048]{1,0:T(8,128)S(1)} fusion(f32[128,2048]{1,0:T(8,128)S(1)} %convolution_add_fusion.1, f32[128,2048]{1,0:T(8,128)S(1)} %convolution_subtract_fusion.1, f32[2048]{0:T(1024)S(1)} %fusion.123, f32[128]{0:T(128)S(1)} %get-tuple-element.52, f32[]{:T(128)} %bitcast.37), kind=kOutput, calls=%fused_computation.146 | convolution fusion | flops 404193280 | bytes 3154436 | tf_op jit(solution)/shard_map/...lc,lm->...mc/dot_general | solution.py:27
  308.5 5.0 fusion.54
  313.5 5.2 %convolution_subtract_fusion = f32[128,2048]{1,0:T(8,128)S(1)} fusion(f32[128,2048]{1,0:T(8,128)S(1)} %fusion.54, f32[128,2048]{1,0:T(8,128)S(1)} %convolution_add_fusion.1, f32[128,2048]{1,0:T(8,128)S(1)} %convolution_subtract_fusion.1, f32[2048]{0:T(1024)S(1)} %fusion.123, f32[128]{0:T(128)S(1)} %get-tuple-element.52, f32[]{:T(128)} %bitcast.37), kind=kOutput, calls=%fused_computation.1 | convolution fusion | flops 404455424 | bytes 4203012 | tf_op jit(solution)/shard_map/...lc,lm->...mc/dot_general | solution.py:24
  318.7 5.3 %multiply_add_fusion = (f32[128,2048]{1,0:T(8,128)S(1)}, f32[128,2048]{1,0:T(8,128)S(1)}) fusion(f32[128,2048]{1,0:T(8,128)S(1)} %convolution_subtract_fusion, f32[128]{0:T(128)S(1)} %get-tuple-element.54, f32[128]{0:T(128)S(1)} %get-tuple-element.55, f32[128,2048]{1,0:T(8,128)S(1)} %fusion.55, f32[128,2048]{1,0:T(8,128)S(1)} %convolution_add_fusion.1, ...), kind=kOutput, calls=%fused_computation.79 | convolution fusion | flops 406028288 | bytes 6301188 | tf_op jit(solution)/shard_map/...lc,lm->...mc/dot_general | solution.py:27
  324.7 3.8 collective-permute-done.4
  332.3 46.9 %collective-permute-done.5 = f32[1,2,128,2048]{3,2,1,0:T(8,128)} collective-permute-done((f32[1,2,128,2048]{3,2,1,0:T(8,128)}, f32[1,2,128,2048]{3,2,1,0:T(8,128)}, u32[]{:S(2)}, u32[]{:S(2)}) %collective-permute-start.5) | collective-permute-done | bytes 2097184 | tf_op jit(solution)/shard_map/ppermute | solution.py:11
  379.1 3.4 multiply_bitcast_fusion.3
  384.6 48.1 %collective-permute-done.6 = f32[1,2,128,2048]{3,2,1,0:T(8,128)S(1)} collective-permute-done((f32[1,2,128,2048]{3,2,1,0:T(8,128)}, f32[1,2,128,2048]{3,2,1,0:T(8,128)S(1)}, u32[]{:S(2)}, u32[]{:S(2)}) %collective-permute-start.6) | collective-permute-done | bytes 2097184 | tf_op jit(solution)/shard_map/ppermute | solution.py:11
  434.1 2.7 multiply_bitcast_fusion.1
  438.2 4.7 collective-permute-start.7
  443.2 45.7 %collective-permute-done.7 = f32[1,2,128,2048]{3,2,1,0:T(8,128)} collective-permute-done((f32[1,2,128,2048]{3,2,1,0:T(8,128)}, f32[1,2,128,2048]{3,2,1,0:T(8,128)}, u32[]{:S(2)}, u32[]{:S(2)}) %collective-permute-start.7) | collective-permute-done | bytes 2097184 | tf_op jit(solution)/shard_map/ppermute | solution.py:11
  488.8 3.3 fusion.14
  492.2 1.5 copy.76
  493.7 2.6 fusion.35
  496.4 1.7 fusion.33
  498.4 2.9 fusion.5
  501.3 2.1 add_bitcast_fusion
  503.4 1.6 fusion.29
  505.0 1.6 fusion.27
  506.6 1.8 fusion.3
  509.1 1.6 fusion.1
  511.5 1.8 copy.88
  (50 shorter events, 30.9 us)
Async XLA Ops:
  2.6 56.0 %all-to-all-start = ((f32[16,2,128,128]{2,3,1,0:T(8,128)}), f32[16,2,128,128]{2,3,1,0:T(8,128)S(1)}, u32[]{:S(2)}, u32[]{:S(2)}) async-start(f32[16,2,128,128]{2,3,1,0:T(8,128)} %stack.36), calls=%async_computation | async-start | bytes 4194304 | tf_op jit(solution)/shard_map/all_to_all | solution.py:83
  58.7 4.4 copy-start.3
  85.1 95.5 %collective-permute-start = (f32[1,2,128,2048]{3,2,1,0:T(8,128)}, f32[1,2,128,2048]{3,2,1,0:T(8,128)}, u32[]{:S(2)}, u32[]{:S(2)}) collective-permute-start(f32[1,2,128,2048]{3,2,1,0:T(8,128)} %pad_maximum_fusion), channel_id=1, source_target_pairs={{0,8},{1,9},{2,10},{3,11},{4,12},{5,13},{6,14},{7,15},{8,0},{9,1},... | collective-permute-start | bytes 6291464 | tf_op jit(solution)/shard_map/ppermute | solution.py:11
  182.5 1.0 copy-start
  183.5 49.2 %collective-permute-start.1 = (f32[1,2,128,2048]{3,2,1,0:T(8,128)S(1)}, f32[1,2,128,2048]{3,2,1,0:T(8,128)}, u32[]{:S(2)}, u32[]{:S(2)}) collective-permute-start(f32[1,2,128,2048]{3,2,1,0:T(8,128)S(1)} %pad_maximum_fusion.1), channel_id=1, source_target_pairs={{0,4},{1,5},{2,6},{3,7},{4,0},{5,1},{6,2},{7,3},{8,12},{9,13},{10,... | collective-permute-start | bytes 6291464 | tf_op jit(solution)/shard_map/ppermute | solution.py:11
  236.4 47.0 %collective-permute-start.2 = (f32[1,2,128,2048]{3,2,1,0:T(8,128)}, f32[1,2,128,2048]{3,2,1,0:T(8,128)}, u32[]{:S(2)}, u32[]{:S(2)}) collective-permute-start(f32[1,2,128,2048]{3,2,1,0:T(8,128)} %pad_maximum_fusion.2), channel_id=1, source_target_pairs={{0,2},{1,3},{2,0},{3,1},{4,6},{5,7},{6,4},{7,5},{8,10},{9,11},{10,... | collective-permute-start | bytes 6291464 | tf_op jit(solution)/shard_map/ppermute | solution.py:11
  285.4 2.5 copy-start.1
  286.8 6.1 %collective-permute-start.3 = (f32[1,2,128,2048]{3,2,1,0:T(8,128)}, f32[1,2,128,2048]{3,2,1,0:T(8,128)}, u32[]{:S(2)}, u32[]{:S(2)}) collective-permute-start(f32[1,2,128,2048]{3,2,1,0:T(8,128)} %pad_maximum_fusion.3), channel_id=1, source_target_pairs={{0,1},{1,0},{2,3},{3,2},{4,5},{5,4},{6,7},{7,6},{8,9},{9,8},{10,11... | collective-permute-start | bytes 6291464 | tf_op jit(solution)/shard_map/ppermute | solution.py:11
  287.9 1.2 copy-start.2
  324.2 4.3 collective-permute-start.4
  330.9 48.2 %collective-permute-start.5 = (f32[1,2,128,2048]{3,2,1,0:T(8,128)}, f32[1,2,128,2048]{3,2,1,0:T(8,128)}, u32[]{:S(2)}, u32[]{:S(2)}) collective-permute-start(f32[1,2,128,2048]{3,2,1,0:T(8,128)} %pad_maximum_fusion.5), channel_id=1, source_target_pairs={{0,2},{1,3},{2,0},{3,1},{4,6},{5,7},{6,4},{7,5},{8,10},{9,11},{10,... | collective-permute-start | bytes 6291464 | tf_op jit(solution)/shard_map/ppermute | solution.py:11
  383.9 48.8 %collective-permute-start.6 = (f32[1,2,128,2048]{3,2,1,0:T(8,128)}, f32[1,2,128,2048]{3,2,1,0:T(8,128)S(1)}, u32[]{:S(2)}, u32[]{:S(2)}) collective-permute-start(f32[1,2,128,2048]{3,2,1,0:T(8,128)} %pad_maximum_fusion.6), channel_id=1, source_target_pairs={{0,4},{1,5},{2,6},{3,7},{4,0},{5,1},{6,2},{7,3},{8,12},{9,13},{10,... | collective-permute-start | bytes 6291464 | tf_op jit(solution)/shard_map/ppermute | solution.py:11
  432.8 1.3 copy-start.4
  438.2 50.6 %collective-permute-start.7 = (f32[1,2,128,2048]{3,2,1,0:T(8,128)}, f32[1,2,128,2048]{3,2,1,0:T(8,128)}, u32[]{:S(2)}, u32[]{:S(2)}) collective-permute-start(f32[1,2,128,2048]{3,2,1,0:T(8,128)} %pad_maximum_fusion.7), channel_id=1, source_target_pairs={{0,8},{1,9},{2,10},{3,11},{4,12},{5,13},{6,14},{7,15},{8,0},{9,1},... | collective-permute-start | bytes 6291464 | tf_op jit(solution)/shard_map/ppermute | solution.py:11
